TPU v7x, 512 devices: a whole 4x4x16 slice. The times are simulated.
512 devices in a mesh: lat: 32 (over z, x_lo), lon: 16 (over y, x_hi, core).
Axes of the slice: x: 4 (x_hi: 2, x_lo: 2; x = x_hi * 2 + x_lo), y: 4, z: 16, core: 2. Of those that a mesh axis runs over, the one named last changes fastest.
Arguments:
- observed: float32 [4096, 8192], P(('lat', 'lon')), may hold values from -12 to 12
- gauged: int32 [4096, 8192], P('lat', 'lon'), may hold values from 0 to 1, as said below
Outputs:
- coarsest_coeffs: float32 [512, 1024], P('lat', 'lon')
- coarse_coeffs: float32 [1024, 2048], P('lat', 'lon')
- fine_coeffs: float32 [2048, 4096], P('lat', 'lon')
- finest_coeffs: float32 [4096, 8192], P('lat', 'lon')
- imputed: float32 [4096, 8192], P(('lat', 'lon'))
Inputs may be any that keep to these rules, and one draw needn't show every extreme that they name: 1 marks a gauged cell.
All inputs are finite; a program needn't handle non-finite values.
Results may differ from a plain program's by a relative error of at most 0.00029.
Values sent between devices are 32-bit elements; how exact they have to be, the bound alone decides.
A program may use at most 64 MiB of HBM per device.

v0:
```python
import math
import jax
import jax.numpy as jnp
from jax import lax
from jax.sharding import PartitionSpec as P

LEVELS = 4
ITERS = 2
highest = lax.Precision.HIGHEST
data_weight = 2.0
kappa_term = 5.0
level_scales = (0.02, 0.03, 0.05, 0.08)


def with_halo(x, sides, width):
    for axis, dim in sides:
        size, length = (lax.axis_size(axis), x.shape[dim])
        up = [(i, (i + 1) % size) for i in range(size - 1)]
        down = [(j, i) for i, j in up]
        last = lax.slice_in_dim(x, length - width, length, axis=dim)
        first = lax.slice_in_dim(x, 0, width, axis=dim)
        before = lax.ppermute(last, axis, up)
        after = lax.ppermute(first, axis, down)
        x = jnp.concatenate([before, x, after], axis=dim)
    return x


def wendland(distance):
    remain = jnp.maximum(1.0 - distance, 0.0)
    return remain**6 * (35.0 * distance * distance + 18.0 * distance + 3.0) / 3.0


def basis_table(cell_total, node_total, spacing, cell_margin, node_margin):
    shape_full = (cell_total + 2 * cell_margin, node_total + 2 * node_margin)
    cell_idx = lax.broadcasted_iota(jnp.int32, shape_full, 0) - cell_margin
    node_idx = lax.broadcasted_iota(jnp.int32, shape_full, 1) - node_margin
    numerator = jnp.abs(2 * cell_idx - 2 * spacing * node_idx - (spacing - 1))
    return wendland(numerator.astype(jnp.float32) / (5.0 * spacing)) / math.sqrt(spacing)


def matmul(left, right):
    return jnp.dot(left, right, precision=highest, preferred_element_type=jnp.float32)


def stencil(values):
    beside = values[2:, 1:-1] + values[:-2, 1:-1] + values[1:-1, 2:] + values[1:-1, :-2]
    return kappa_term * values[1:-1, 1:-1] - beside


def level_products(first, second):
    accum = jnp.float32(0.0)
    for level_idx in range(len(first)):
        accum = accum + jnp.sum(first[level_idx] * second[level_idx])
    return accum


def norm_sum(residual):
    return lax.psum(level_products(residual, residual), ("lat", "lon"))


def body(observed, gauged):
    tiled = lax.all_to_all(observed, "lon", split_axis=1, concat_axis=0, tiled=True)
    lat_index = lax.axis_index("lat")
    lon_index = lax.axis_index("lon")
    lat_total = lax.axis_size("lat")
    lon_total = lax.axis_size("lon")
    rows_here, cols_here = gauged.shape
    gauge_float = gauged.astype(jnp.float32)
    spacings = [2 ** (LEVELS - 1 - level_idx) for level_idx in range(LEVELS)]
    node_shapes = [(rows_here // sp, cols_here // sp) for sp in spacings]
    fwd_lat = [basis_table(rows_here, node_shapes[k][0], spacings[k], 0, 2) for k in range(LEVELS)]
    fwd_lon = [basis_table(cols_here, node_shapes[k][1], spacings[k], 0, 2) for k in range(LEVELS)]
    valid_nodes = []
    for k in range(LEVELS):
        node_rows, node_cols = node_shapes[k]
        row_global = (
            lat_index * node_rows + lax.broadcasted_iota(jnp.int32, (node_rows + 2, 1), 0) - 1
        )
        col_global = (
            lon_index * node_cols + lax.broadcasted_iota(jnp.int32, (1, node_cols + 2), 1) - 1
        )
        row_valid = (row_global >= 0) & (row_global < node_rows * lat_total)
        col_valid = (col_global >= 0) & (col_global < node_cols * lon_total)
        valid_nodes.append((row_valid & col_valid).astype(jnp.float32))

    def synthesize(coeffs):
        surface = jnp.zeros((rows_here, cols_here), jnp.float32)
        extended_all = []
        for k in range(LEVELS):
            extended = with_halo(coeffs[k], (("lat", 0), ("lon", 1)), 2)
            surface = surface + matmul(matmul(fwd_lat[k], extended), fwd_lon[k].T)
            extended_all.append(extended)
        return (surface, extended_all)

    def adjoint(misfit):
        result = []
        widened = with_halo(misfit, (("lat", 0), ("lon", 1)), 16)
        for k in range(LEVELS):
            back_lat = basis_table(rows_here, node_shapes[k][0], spacings[k], 16, 0).T
            back_lon = basis_table(cols_here, node_shapes[k][1], spacings[k], 16, 0)
            result.append(matmul(matmul(back_lat, widened), back_lon))
        return result

    right_side = adjoint(data_weight * gauge_float * tiled)
    solution = [jnp.zeros_like(piece) for piece in right_side]
    surface_sum = jnp.zeros((rows_here, cols_here), jnp.float32)
    residual = right_side
    search = right_side
    res_norm = norm_sum(residual)
    for iteration in range(ITERS):
        apply_surface, apply_extended_all = synthesize(search)
        backs = adjoint(data_weight * gauge_float * apply_surface)
        curv_local = data_weight * jnp.sum(gauge_float * apply_surface * apply_surface)
        images = []
        for apply_k in range(LEVELS):
            smoothed = stencil(apply_extended_all[apply_k]) * valid_nodes[apply_k]
            images.append(backs[apply_k] + level_scales[apply_k] * stencil(smoothed))
            own_part = smoothed[1:-1, 1:-1]
            curv_local = curv_local + level_scales[apply_k] * jnp.sum(own_part * own_part)
        images, surface, curv_local = (images, apply_surface, curv_local)
        curv_sum = lax.psum(curv_local, ("lat", "lon"))
        step_size = res_norm / curv_sum
        solution = [solution[k] + step_size * search[k] for k in range(LEVELS)]
        surface_sum = surface_sum + step_size * surface
        if iteration + 1 < ITERS:
            residual = [residual[k] - step_size * images[k] for k in range(LEVELS)]
            new_norm = norm_sum(residual)
            search = [residual[k] + new_norm / res_norm * search[k] for k in range(LEVELS)]
            res_norm = new_norm
    final_surface, unused_rims = synthesize(solution)
    swath_field = lax.all_to_all(final_surface, "lon", split_axis=0, concat_axis=1, tiled=True)
    return (solution[0], solution[1], solution[2], solution[3], swath_field)


def solution(mesh):
    placed = (P(("lat", "lon"), None), P("lat", "lon"))
    return jax.shard_map(
        body,
        mesh=mesh,
        in_specs=placed,
        out_specs=(
            P("lat", "lon"),
            P("lat", "lon"),
            P("lat", "lon"),
            P("lat", "lon"),
            P(("lat", "lon"), None),
        ),
        check_vma=False,
    )
```

profile of v0, /device:TPU:98, one launch (start us, length us, event | category | flops | bytes accessed | tf_op | source)
XLA Modules:
  0.0 623.4 jit_solution(1043832198746908045)
XLA Ops:
  0.6 6.3 %all-to-all-start = ((f32[8,16,512]{2,0,1:T(8,128)}), f32[8,16,512]{2,0,1:T(8,128)S(1)}, u32[]{:S(2)}, u32[]{:S(2)}) async-start(f32[8,16,512]{2,0,1:T(8,128)} %bitcast.39), calls=%async_computation | async-start | bytes 524288 | tf_op jit(solution)/shard_map/all_to_all | solution.py:62
  7.4 9.0 %all-to-all-done = f32[8,16,512]{2,0,1:T(8,128)S(1)} async-done(((f32[8,16,512]{2,0,1:T(8,128)}), f32[8,16,512]{2,0,1:T(8,128)S(1)}, u32[]{:S(2)}, u32[]{:S(2)}) %all-to-all-start) | async-done | bytes 262176 | tf_op jit(solution)/shard_map/all_to_all | solution.py:62
  16.5 3.3 collective-permute-start.1
  19.9 4.6 collective-permute-start
  27.4 3.0 collective-permute-start.2
  32.9 2.5 collective-permute-start.5
  35.5 5.7 collective-permute-start.4
  45.1 6.0 collective-permute-start.12
  55.4 2.3 multiply_reduce_fusion.2
  59.8 2.7 collective-permute-start.6
  64.4 5.8 collective-permute-start.8
  75.6 8.3 %collective-permute-start.10 = (f32[36,2]{1,0:T(8,128)S(1)}, f32[36,2]{1,0:T(8,128)S(1)}, u32[]{:S(2)}, u32[]{:S(2)}) collective-permute-start(f32[36,2]{1,0:T(8,128)S(1)} %get-tuple-element.54), channel_id=1, source_target_pairs={{0,1},{1,2},{2,3},{3,4},{4,5},{5,6},{6,7},{7,8},{8,9},{9,10},{10,1... | collective-permute-start | bytes 872 | tf_op jit(solution)/shard_map/ppermute | solution.py:22
  84.5 5.8 collective-permute-start.16
  92.3 6.1 collective-permute-start.14
  104.4 6.2 %collective-permute-start.18 = (f32[132,2]{1,0:T(8,128)S(1)}, f32[132,2]{1,0:T(8,128)S(1)}, u32[]{:S(2)}, u32[]{:S(2)}) collective-permute-start(f32[132,2]{1,0:T(8,128)S(1)} %get-tuple-element.20), channel_id=1, source_target_pairs={{0,1},{1,2},{2,3},{3,4},{4,5},{5,6},{6,7},{7,8},{8,9},{9,10},{10,1... | collective-permute-start | bytes 3176 | tf_op jit(solution)/shard_map/ppermute | solution.py:22
  112.8 2.8 fusion.106
  117.5 6.0 collective-permute-start.20
  127.5 5.5 collective-permute-start.22
  133.1 109.8 %all-reduce = (f32[]{:T(128)}, f32[]{:T(128)}) all-reduce(f32[]{:T(128)S(6)} %add.627, f32[]{:T(128)S(6)} %add.678), channel_id=1, replica_groups=mesh['lat'=32,'lon'=16] {'lat','lon'}, use_global_device_ids=true, to_apply=%region_4.0 | all-reduce | flops 2 | bytes 16 | tf_op jit(solution)/shard_map/psum | solution.py:58
  250.2 2.3 multiply_reduce_fusion
  255.2 102.0 %psum.30 = f32[]{:T(128)} all-reduce(f32[]{:T(128)S(6)} %add.697), channel_id=1, replica_groups=mesh['lat'=32,'lon'=16] {'lat','lon'}, use_global_device_ids=true, to_apply=%region_15.0 | all-reduce | flops 1 | bytes 8 | tf_op jit(solution)/shard_map/psum | solution.py:58
  358.6 2.7 collective-permute-start.33
  361.3 5.3 collective-permute-start.32
  366.6 1.9 collective-permute-start.25
  368.5 6.0 collective-permute-start.24
  374.5 1.9 collective-permute-start.29
  377.9 3.0 collective-permute-start.26
  381.0 6.0 collective-permute-start.28
  387.0 1.9 collective-permute-start.37
  391.5 4.7 collective-permute-start.30
  397.6 5.8 collective-permute-start.36
  405.4 5.5 collective-permute-start.34
  416.8 5.8 collective-permute-start.38
  425.2 2.8 fusion.48
  430.5 104.2 %psum.31 = f32[]{:T(128)} all-reduce(f32[]{:T(128)S(6)} %add.720), channel_id=1, replica_groups=mesh['lat'=32,'lon'=16] {'lat','lon'}, use_global_device_ids=true, to_apply=%region_21.0 | all-reduce | flops 1 | bytes 8 | tf_op jit(solution)/shard_map/psum | solution.py:121
  536.2 4.4 collective-permute-start.49
  540.6 3.5 collective-permute-start.48
  544.2 2.3 collective-permute-start.41
  546.5 5.6 collective-permute-start.40
  552.2 1.9 collective-permute-start.45
  555.5 3.0 collective-permute-start.42
  558.6 6.0 collective-permute-start.44
  567.6 6.0 collective-permute-start.52
  575.0 4.0 collective-permute-start.46
  580.4 5.8 collective-permute-start.50
  590.3 6.2 collective-permute-start.54
  598.2 2.2 fusion.7
  600.5 22.0 %all_to_all.38 = f32[16,8,512]{2,1,0:T(8,128)S(1)} all-to-all(f32[16,8,512]{2,1,0:T(8,128)S(1)} %fusion.7), channel_id=1, replica_groups=mesh['lat'=32,'lon'=16] {'lon'}, dimensions={0} | all-to-all | bytes 524288 | tf_op jit(solution)/shard_map/all_to_all | solution.py:131
  (221 shorter events, 68.4 us)
Async XLA Ops:
  0.6 15.8 %all-to-all-start = ((f32[8,16,512]{2,0,1:T(8,128)}), f32[8,16,512]{2,0,1:T(8,128)S(1)}, u32[]{:S(2)}, u32[]{:S(2)}) async-start(f32[8,16,512]{2,0,1:T(8,128)} %bitcast.39), calls=%async_computation | async-start | bytes 524288 | tf_op jit(solution)/shard_map/all_to_all | solution.py:62
  16.5 8.0 %collective-permute-start.1 = (f32[16,512]{1,0:T(8,128)S(1)}, f32[16,512]{1,0:T(8,128)S(1)}, u32[]{:S(2)}, u32[]{:S(2)}) collective-permute-start(f32[16,512]{1,0:T(8,128)S(1)} %get-tuple-element.31), channel_id=1, source_target_pairs={{16,0},{32,16},{48,32},{64,48},{80,64},{96,80},{112,96},{128,112},... | collective-permute-start | bytes 98312 | tf_op jit(solution)/shard_map/ppermute | solution.py:23
  32.9 26.8 %collective-permute-start.5 = (f32[2,64]{1,0:T(2,128)S(1)}, f32[2,64]{1,0:T(2,128)S(1)}, u32[]{:S(2)}, u32[]{:S(2)}) collective-permute-start(f32[2,64]{1,0:T(2,128)S(1)} %get-tuple-element.76), channel_id=1, source_target_pairs={{16,0},{32,16},{48,32},{64,48},{80,64},{96,80},{112,96},{128,112},... | collective-permute-start | bytes 1544 | tf_op jit(solution)/shard_map/ppermute | solution.py:23
  35.5 24.2 %collective-permute-start.4 = (f32[2,64]{1,0:T(2,128)S(1)}, f32[2,64]{1,0:T(2,128)S(1)}, u32[]{:S(2)}, u32[]{:S(2)}) collective-permute-start(f32[2,64]{1,0:T(2,128)S(1)} %get-tuple-element.75), channel_id=1, source_target_pairs={{0,16},{16,32},{32,48},{48,64},{64,80},{80,96},{96,112},{112,128},... | collective-permute-start | bytes 1544 | tf_op jit(solution)/shard_map/ppermute | solution.py:22
  43.2 47.7 %collective-permute-start.13 = (f32[2,256]{1,0:T(2,128)S(1)}, f32[2,256]{1,0:T(2,128)S(1)}, u32[]{:S(2)}, u32[]{:S(2)}) collective-permute-start(f32[2,256]{1,0:T(2,128)S(1)} %get-tuple-element.46), channel_id=1, source_target_pairs={{16,0},{32,16},{48,32},{64,48},{80,64},{96,80},{112,96},{128,112},... | collective-permute-start | bytes 6152 | tf_op jit(solution)/shard_map/ppermute | solution.py:23
  45.1 45.8 %collective-permute-start.12 = (f32[2,256]{1,0:T(2,128)S(1)}, f32[2,256]{1,0:T(2,128)S(1)}, u32[]{:S(2)}, u32[]{:S(2)}) collective-permute-start(f32[2,256]{1,0:T(2,128)S(1)} %get-tuple-element.45), channel_id=1, source_target_pairs={{0,16},{16,32},{32,48},{48,64},{64,80},{80,96},{96,112},{112,128},... | collective-permute-start | bytes 6152 | tf_op jit(solution)/shard_map/ppermute | solution.py:22
  52.8 20.7 %collective-permute-start.9 = (f32[2,128]{1,0:T(2,128)S(1)}, f32[2,128]{1,0:T(2,128)S(1)}, u32[]{:S(2)}, u32[]{:S(2)}) collective-permute-start(f32[2,128]{1,0:T(2,128)S(1)} %get-tuple-element.61), channel_id=1, source_target_pairs={{16,0},{32,16},{48,32},{64,48},{80,64},{96,80},{112,96},{128,112},... | collective-permute-start | bytes 3080 | tf_op jit(solution)/shard_map/ppermute | solution.py:23
  63.1 7.3 %collective-permute-start.7 = (f32[20,2]{1,0:T(8,128)S(1)}, f32[20,2]{1,0:T(8,128)S(1)}, u32[]{:S(2)}, u32[]{:S(2)}) collective-permute-start(f32[20,2]{1,0:T(8,128)S(1)} %get-tuple-element.70), channel_id=1, source_target_pairs={{1,0},{2,1},{3,2},{4,3},{5,4},{6,5},{7,6},{8,7},{9,8},{10,9},{11,1... | collective-permute-start | bytes 488 | tf_op jit(solution)/shard_map/ppermute | solution.py:23
  64.4 9.1 %collective-permute-start.8 = (f32[2,128]{1,0:T(2,128)S(1)}, f32[2,128]{1,0:T(2,128)S(1)}, u32[]{:S(2)}, u32[]{:S(2)}) collective-permute-start(f32[2,128]{1,0:T(2,128)S(1)} %get-tuple-element.60), channel_id=1, source_target_pairs={{0,16},{16,32},{32,48},{48,64},{64,80},{80,96},{96,112},{112,128},... | collective-permute-start | bytes 3080 | tf_op jit(solution)/shard_map/ppermute | solution.py:22
  70.4 32.6 %collective-permute-start.17 = (f32[2,512]{1,0:T(2,128)S(1)}, f32[2,512]{1,0:T(2,128)S(1)}, u32[]{:S(2)}, u32[]{:S(2)}) collective-permute-start(f32[2,512]{1,0:T(2,128)S(1)} %get-tuple-element.29), channel_id=1, source_target_pairs={{16,0},{32,16},{48,32},{64,48},{80,64},{96,80},{112,96},{128,112},... | collective-permute-start | bytes 12296 | tf_op jit(solution)/shard_map/ppermute | solution.py:23
  73.6 10.9 %collective-permute-start.11 = (f32[36,2]{1,0:T(8,128)S(1)}, f32[36,2]{1,0:T(8,128)S(1)}, u32[]{:S(2)}, u32[]{:S(2)}) collective-permute-start(f32[36,2]{1,0:T(8,128)S(1)} %get-tuple-element.55), channel_id=1, source_target_pairs={{1,0},{2,1},{3,2},{4,3},{5,4},{6,5},{7,6},{8,7},{9,8},{10,9},{11,1... | collective-permute-start | bytes 872 | tf_op jit(solution)/shard_map/ppermute | solution.py:23
  75.6 14.7 %collective-permute-start.10 = (f32[36,2]{1,0:T(8,128)S(1)}, f32[36,2]{1,0:T(8,128)S(1)}, u32[]{:S(2)}, u32[]{:S(2)}) collective-permute-start(f32[36,2]{1,0:T(8,128)S(1)} %get-tuple-element.54), channel_id=1, source_target_pairs={{0,1},{1,2},{2,3},{3,4},{4,5},{5,6},{6,7},{7,8},{8,9},{9,10},{10,1... | collective-permute-start | bytes 872 | tf_op jit(solution)/shard_map/ppermute | solution.py:22
  84.5 18.5 %collective-permute-start.16 = (f32[2,512]{1,0:T(2,128)S(1)}, f32[2,512]{1,0:T(2,128)S(1)}, u32[]{:S(2)}, u32[]{:S(2)}) collective-permute-start(f32[2,512]{1,0:T(2,128)S(1)} %get-tuple-element.28), channel_id=1, source_target_pairs={{0,16},{16,32},{32,48},{48,64},{64,80},{80,96},{96,112},{112,128},... | collective-permute-start | bytes 12296 | tf_op jit(solution)/shard_map/ppermute | solution.py:22
  91.0 8.7 %collective-permute-start.15 = (f32[68,2]{1,0:T(8,128)S(1)}, f32[68,2]{1,0:T(8,128)S(1)}, u32[]{:S(2)}, u32[]{:S(2)}) collective-permute-start(f32[68,2]{1,0:T(8,128)S(1)} %get-tuple-element.40), channel_id=1, source_target_pairs={{1,0},{2,1},{3,2},{4,3},{5,4},{6,5},{7,6},{8,7},{9,8},{10,9},{11,1... | collective-permute-start | bytes 1640 | tf_op jit(solution)/shard_map/ppermute | solution.py:23
  92.3 7.4 %collective-permute-start.14 = (f32[68,2]{1,0:T(8,128)S(1)}, f32[68,2]{1,0:T(8,128)S(1)}, u32[]{:S(2)}, u32[]{:S(2)}) collective-permute-start(f32[68,2]{1,0:T(8,128)S(1)} %get-tuple-element.39), channel_id=1, source_target_pairs={{0,1},{1,2},{2,3},{3,4},{4,5},{5,6},{6,7},{7,8},{8,9},{9,10},{10,1... | collective-permute-start | bytes 1640 | tf_op jit(solution)/shard_map/ppermute | solution.py:22
  103.1 8.9 %collective-permute-start.19 = (f32[132,2]{1,0:T(8,128)S(1)}, f32[132,2]{1,0:T(8,128)S(1)}, u32[]{:S(2)}, u32[]{:S(2)}) collective-permute-start(f32[132,2]{1,0:T(8,128)S(1)} %get-tuple-element.21), channel_id=1, source_target_pairs={{1,0},{2,1},{3,2},{4,3},{5,4},{6,5},{7,6},{8,7},{9,8},{10,9},{11,1... | collective-permute-start | bytes 3176 | tf_op jit(solution)/shard_map/ppermute | solution.py:23
  104.4 7.6 %collective-permute-start.18 = (f32[132,2]{1,0:T(8,128)S(1)}, f32[132,2]{1,0:T(8,128)S(1)}, u32[]{:S(2)}, u32[]{:S(2)}) collective-permute-start(f32[132,2]{1,0:T(8,128)S(1)} %get-tuple-element.20), channel_id=1, source_target_pairs={{0,1},{1,2},{2,3},{3,4},{4,5},{5,6},{6,7},{7,8},{8,9},{9,10},{10,1... | collective-permute-start | bytes 3176 | tf_op jit(solution)/shard_map/ppermute | solution.py:22
  115.6 10.5 %collective-permute-start.21 = (f32[16,512]{1,0:T(8,128)S(1)}, f32[16,512]{1,0:T(8,128)S(1)}, u32[]{:S(2)}, u32[]{:S(2)}) collective-permute-start(f32[16,512]{1,0:T(8,128)S(1)} %get-tuple-element.27), channel_id=1, source_target_pairs={{16,0},{32,16},{48,32},{64,48},{80,64},{96,80},{112,96},{128,112},... | collective-permute-start | bytes 98312 | tf_op jit(solution)/shard_map/ppermute | solution.py:23
  117.5 8.6 %collective-permute-start.20 = (f32[16,512]{1,0:T(8,128)S(1)}, f32[16,512]{1,0:T(8,128)S(1)}, u32[]{:S(2)}, u32[]{:S(2)}) collective-permute-start(f32[16,512]{1,0:T(8,128)S(1)} %get-tuple-element.26), channel_id=1, source_target_pairs={{0,16},{16,32},{32,48},{48,64},{64,80},{80,96},{96,112},{112,128},... | collective-permute-start | bytes 98312 | tf_op jit(solution)/shard_map/ppermute | solution.py:22
  126.2 118.1 %collective-permute-start.23 = (f32[160,16]{1,0:T(8,128)S(1)}, f32[160,16]{1,0:T(8,128)S(1)}, u32[]{:S(2)}, u32[]{:S(2)}) collective-permute-start(f32[160,16]{1,0:T(8,128)S(1)} %get-tuple-element.13), channel_id=1, source_target_pairs={{1,0},{2,1},{3,2},{4,3},{5,4},{6,5},{7,6},{8,7},{9,8},{10,9},{11,1... | collective-permute-start | bytes 30728 | tf_op jit(solution)/shard_map/ppermute | solution.py:23
  127.5 116.8 %collective-permute-start.22 = (f32[160,16]{1,0:T(8,128)S(1)}, f32[160,16]{1,0:T(8,128)S(1)}, u32[]{:S(2)}, u32[]{:S(2)}) collective-permute-start(f32[160,16]{1,0:T(8,128)S(1)} %get-tuple-element.12), channel_id=1, source_target_pairs={{0,1},{1,2},{2,3},{3,4},{4,5},{5,6},{6,7},{7,8},{8,9},{9,10},{10,1... | collective-permute-start | bytes 30728 | tf_op jit(solution)/shard_map/ppermute | solution.py:22
  358.6 45.4 %collective-permute-start.33 = (f32[2,256]{1,0:T(2,128)S(1)}, f32[2,256]{1,0:T(2,128)S(1)}, u32[]{:S(2)}, u32[]{:S(2)}) collective-permute-start(f32[2,256]{1,0:T(2,128)S(1)} %get-tuple-element.44), channel_id=1, source_target_pairs={{16,0},{32,16},{48,32},{64,48},{80,64},{96,80},{112,96},{128,112},... | collective-permute-start | bytes 6152 | tf_op jit(solution)/shard_map/ppermute | solution.py:23
  361.3 42.7 %collective-permute-start.32 = (f32[2,256]{1,0:T(2,128)S(1)}, f32[2,256]{1,0:T(2,128)S(1)}, u32[]{:S(2)}, u32[]{:S(2)}) collective-permute-start(f32[2,256]{1,0:T(2,128)S(1)} %get-tuple-element.43), channel_id=1, source_target_pairs={{0,16},{16,32},{32,48},{48,64},{64,80},{80,96},{96,112},{112,128},... | collective-permute-start | bytes 6152 | tf_op jit(solution)/shard_map/ppermute | solution.py:22
  366.6 10.0 %collective-permute-start.25 = (f32[2,64]{1,0:T(2,128)S(1)}, f32[2,64]{1,0:T(2,128)S(1)}, u32[]{:S(2)}, u32[]{:S(2)}) collective-permute-start(f32[2,64]{1,0:T(2,128)S(1)} %get-tuple-element.74), channel_id=1, source_target_pairs={{16,0},{32,16},{48,32},{64,48},{80,64},{96,80},{112,96},{128,112},... | collective-permute-start | bytes 1544 | tf_op jit(solution)/shard_map/ppermute | solution.py:23
  368.5 8.1 %collective-permute-start.24 = (f32[2,64]{1,0:T(2,128)S(1)}, f32[2,64]{1,0:T(2,128)S(1)}, u32[]{:S(2)}, u32[]{:S(2)}) collective-permute-start(f32[2,64]{1,0:T(2,128)S(1)} %get-tuple-element.73), channel_id=1, source_target_pairs={{0,16},{16,32},{32,48},{48,64},{64,80},{80,96},{96,112},{112,128},... | collective-permute-start | bytes 1544 | tf_op jit(solution)/shard_map/ppermute | solution.py:22
  374.5 15.6 %collective-permute-start.29 = (f32[2,128]{1,0:T(2,128)S(1)}, f32[2,128]{1,0:T(2,128)S(1)}, u32[]{:S(2)}, u32[]{:S(2)}) collective-permute-start(f32[2,128]{1,0:T(2,128)S(1)} %get-tuple-element.59), channel_id=1, source_target_pairs={{16,0},{32,16},{48,32},{64,48},{80,64},{96,80},{112,96},{128,112},... | collective-permute-start | bytes 3080 | tf_op jit(solution)/shard_map/ppermute | solution.py:23
  377.9 9.1 %collective-permute-start.26 = (f32[20,2]{1,0:T(8,128)S(1)}, f32[20,2]{1,0:T(8,128)S(1)}, u32[]{:S(2)}, u32[]{:S(2)}) collective-permute-start(f32[20,2]{1,0:T(8,128)S(1)} %get-tuple-element.67), channel_id=1, source_target_pairs={{0,1},{1,2},{2,3},{3,4},{4,5},{5,6},{6,7},{7,8},{8,9},{9,10},{10,1... | collective-permute-start | bytes 488 | tf_op jit(solution)/shard_map/ppermute | solution.py:22
  381.0 9.1 %collective-permute-start.28 = (f32[2,128]{1,0:T(2,128)S(1)}, f32[2,128]{1,0:T(2,128)S(1)}, u32[]{:S(2)}, u32[]{:S(2)}) collective-permute-start(f32[2,128]{1,0:T(2,128)S(1)} %get-tuple-element.58), channel_id=1, source_target_pairs={{0,16},{16,32},{32,48},{48,64},{64,80},{80,96},{96,112},{112,128},... | collective-permute-start | bytes 3080 | tf_op jit(solution)/shard_map/ppermute | solution.py:22
  387.0 28.4 %collective-permute-start.37 = (f32[2,512]{1,0:T(2,128)S(1)}, f32[2,512]{1,0:T(2,128)S(1)}, u32[]{:S(2)}, u32[]{:S(2)}) collective-permute-start(f32[2,512]{1,0:T(2,128)S(1)} %get-tuple-element.25), channel_id=1, source_target_pairs={{16,0},{32,16},{48,32},{64,48},{80,64},{96,80},{112,96},{128,112},... | collective-permute-start | bytes 12296 | tf_op jit(solution)/shard_map/ppermute | solution.py:23
  390.2 7.4 %collective-permute-start.31 = (f32[36,2]{1,0:T(8,128)S(1)}, f32[36,2]{1,0:T(8,128)S(1)}, u32[]{:S(2)}, u32[]{:S(2)}) collective-permute-start(f32[36,2]{1,0:T(8,128)S(1)} %get-tuple-element.53), channel_id=1, source_target_pairs={{1,0},{2,1},{3,2},{4,3},{5,4},{6,5},{7,6},{8,7},{9,8},{10,9},{11,1... | collective-permute-start | bytes 872 | tf_op jit(solution)/shard_map/ppermute | solution.py:23
  391.5 11.8 %collective-permute-start.30 = (f32[36,2]{1,0:T(8,128)S(1)}, f32[36,2]{1,0:T(8,128)S(1)}, u32[]{:S(2)}, u32[]{:S(2)}) collective-permute-start(f32[36,2]{1,0:T(8,128)S(1)} %get-tuple-element.52), channel_id=1, source_target_pairs={{0,1},{1,2},{2,3},{3,4},{4,5},{5,6},{6,7},{7,8},{8,9},{9,10},{10,1... | collective-permute-start | bytes 872 | tf_op jit(solution)/shard_map/ppermute | solution.py:22
  397.6 17.8 %collective-permute-start.36 = (f32[2,512]{1,0:T(2,128)S(1)}, f32[2,512]{1,0:T(2,128)S(1)}, u32[]{:S(2)}, u32[]{:S(2)}) collective-permute-start(f32[2,512]{1,0:T(2,128)S(1)} %get-tuple-element.24), channel_id=1, source_target_pairs={{0,16},{16,32},{32,48},{48,64},{64,80},{80,96},{96,112},{112,128},... | collective-permute-start | bytes 12296 | tf_op jit(solution)/shard_map/ppermute | solution.py:22
  404.1 8.2 %collective-permute-start.35 = (f32[68,2]{1,0:T(8,128)S(1)}, f32[68,2]{1,0:T(8,128)S(1)}, u32[]{:S(2)}, u32[]{:S(2)}) collective-permute-start(f32[68,2]{1,0:T(8,128)S(1)} %get-tuple-element.38), channel_id=1, source_target_pairs={{1,0},{2,1},{3,2},{4,3},{5,4},{6,5},{7,6},{8,7},{9,8},{10,9},{11,1... | collective-permute-start | bytes 1640 | tf_op jit(solution)/shard_map/ppermute | solution.py:23
  415.5 8.5 %collective-permute-start.39 = (f32[132,2]{1,0:T(8,128)S(1)}, f32[132,2]{1,0:T(8,128)S(1)}, u32[]{:S(2)}, u32[]{:S(2)}) collective-permute-start(f32[132,2]{1,0:T(8,128)S(1)} %get-tuple-element.19), channel_id=1, source_target_pairs={{1,0},{2,1},{3,2},{4,3},{5,4},{6,5},{7,6},{8,7},{9,8},{10,9},{11,1... | collective-permute-start | bytes 3176 | tf_op jit(solution)/shard_map/ppermute | solution.py:23
  416.8 7.2 %collective-permute-start.38 = (f32[132,2]{1,0:T(8,128)S(1)}, f32[132,2]{1,0:T(8,128)S(1)}, u32[]{:S(2)}, u32[]{:S(2)}) collective-permute-start(f32[132,2]{1,0:T(8,128)S(1)} %get-tuple-element.18), channel_id=1, source_target_pairs={{0,1},{1,2},{2,3},{3,4},{4,5},{5,6},{6,7},{7,8},{8,9},{9,10},{10,1... | collective-permute-start | bytes 3176 | tf_op jit(solution)/shard_map/ppermute | solution.py:22
  536.2 38.8 %collective-permute-start.49 = (f32[2,256]{1,0:T(2,128)S(1)}, f32[2,256]{1,0:T(2,128)S(1)}, u32[]{:S(2)}, u32[]{:S(2)}) collective-permute-start(f32[2,256]{1,0:T(2,128)S(1)} %get-tuple-element.42), channel_id=1, source_target_pairs={{16,0},{32,16},{48,32},{64,48},{80,64},{96,80},{112,96},{128,112},... | collective-permute-start | bytes 6152 | tf_op jit(solution)/shard_map/ppermute | solution.py:23
  540.6 38.4 %collective-permute-start.48 = (f32[2,256]{1,0:T(2,128)S(1)}, f32[2,256]{1,0:T(2,128)S(1)}, u32[]{:S(2)}, u32[]{:S(2)}) collective-permute-start(f32[2,256]{1,0:T(2,128)S(1)} %get-tuple-element.41), channel_id=1, source_target_pairs={{0,16},{16,32},{32,48},{48,64},{64,80},{80,96},{96,112},{112,128},... | collective-permute-start | bytes 6152 | tf_op jit(solution)/shard_map/ppermute | solution.py:22
  544.2 9.9 %collective-permute-start.41 = (f32[2,64]{1,0:T(2,128)S(1)}, f32[2,64]{1,0:T(2,128)S(1)}, u32[]{:S(2)}, u32[]{:S(2)}) collective-permute-start(f32[2,64]{1,0:T(2,128)S(1)} %get-tuple-element.72), channel_id=1, source_target_pairs={{16,0},{32,16},{48,32},{64,48},{80,64},{96,80},{112,96},{128,112},... | collective-permute-start | bytes 1544 | tf_op jit(solution)/shard_map/ppermute | solution.py:23
  546.5 7.6 %collective-permute-start.40 = (f32[2,64]{1,0:T(2,128)S(1)}, f32[2,64]{1,0:T(2,128)S(1)}, u32[]{:S(2)}, u32[]{:S(2)}) collective-permute-start(f32[2,64]{1,0:T(2,128)S(1)} %get-tuple-element.71), channel_id=1, source_target_pairs={{0,16},{16,32},{32,48},{48,64},{64,80},{80,96},{96,112},{112,128},... | collective-permute-start | bytes 1544 | tf_op jit(solution)/shard_map/ppermute | solution.py:22
  552.2 15.4 %collective-permute-start.45 = (f32[2,128]{1,0:T(2,128)S(1)}, f32[2,128]{1,0:T(2,128)S(1)}, u32[]{:S(2)}, u32[]{:S(2)}) collective-permute-start(f32[2,128]{1,0:T(2,128)S(1)} %get-tuple-element.57), channel_id=1, source_target_pairs={{16,0},{32,16},{48,32},{64,48},{80,64},{96,80},{112,96},{128,112},... | collective-permute-start | bytes 3080 | tf_op jit(solution)/shard_map/ppermute | solution.py:23
  555.5 9.1 %collective-permute-start.42 = (f32[20,2]{1,0:T(8,128)S(1)}, f32[20,2]{1,0:T(8,128)S(1)}, u32[]{:S(2)}, u32[]{:S(2)}) collective-permute-start(f32[20,2]{1,0:T(8,128)S(1)} %get-tuple-element.62), channel_id=1, source_target_pairs={{0,1},{1,2},{2,3},{3,4},{4,5},{5,6},{6,7},{7,8},{8,9},{9,10},{10,1... | collective-permute-start | bytes 488 | tf_op jit(solution)/shard_map/ppermute | solution.py:22
  558.6 15.0 %collective-permute-start.44 = (f32[2,128]{1,0:T(2,128)S(1)}, f32[2,128]{1,0:T(2,128)S(1)}, u32[]{:S(2)}, u32[]{:S(2)}) collective-permute-start(f32[2,128]{1,0:T(2,128)S(1)} %get-tuple-element.56), channel_id=1, source_target_pairs={{0,16},{16,32},{32,48},{48,64},{64,80},{80,96},{96,112},{112,128},... | collective-permute-start | bytes 3080 | tf_op jit(solution)/shard_map/ppermute | solution.py:22
  564.6 24.3 %collective-permute-start.53 = (f32[2,512]{1,0:T(2,128)S(1)}, f32[2,512]{1,0:T(2,128)S(1)}, u32[]{:S(2)}, u32[]{:S(2)}) collective-permute-start(f32[2,512]{1,0:T(2,128)S(1)} %get-tuple-element.23), channel_id=1, source_target_pairs={{16,0},{32,16},{48,32},{64,48},{80,64},{96,80},{112,96},{128,112},... | collective-permute-start | bytes 12296 | tf_op jit(solution)/shard_map/ppermute | solution.py:23
  567.6 21.4 %collective-permute-start.52 = (f32[2,512]{1,0:T(2,128)S(1)}, f32[2,512]{1,0:T(2,128)S(1)}, u32[]{:S(2)}, u32[]{:S(2)}) collective-permute-start(f32[2,512]{1,0:T(2,128)S(1)} %get-tuple-element.22), channel_id=1, source_target_pairs={{0,16},{16,32},{32,48},{48,64},{64,80},{80,96},{96,112},{112,128},... | collective-permute-start | bytes 12296 | tf_op jit(solution)/shard_map/ppermute | solution.py:22
  575.0 11.2 %collective-permute-start.46 = (f32[36,2]{1,0:T(8,128)S(1)}, f32[36,2]{1,0:T(8,128)S(1)}, u32[]{:S(2)}, u32[]{:S(2)}) collective-permute-start(f32[36,2]{1,0:T(8,128)S(1)} %get-tuple-element.50), channel_id=1, source_target_pairs={{0,1},{1,2},{2,3},{3,4},{4,5},{5,6},{6,7},{7,8},{8,9},{9,10},{10,1... | collective-permute-start | bytes 872 | tf_op jit(solution)/shard_map/ppermute | solution.py:22
  579.1 7.5 %collective-permute-start.51 = (f32[68,2]{1,0:T(8,128)S(1)}, f32[68,2]{1,0:T(8,128)S(1)}, u32[]{:S(2)}, u32[]{:S(2)}) collective-permute-start(f32[68,2]{1,0:T(8,128)S(1)} %get-tuple-element.36), channel_id=1, source_target_pairs={{1,0},{2,1},{3,2},{4,3},{5,4},{6,5},{7,6},{8,7},{9,8},{10,9},{11,1... | collective-permute-start | bytes 1640 | tf_op jit(solution)/shard_map/ppermute | solution.py:23
  589.0 8.5 %collective-permute-start.55 = (f32[132,2]{1,0:T(8,128)S(1)}, f32[132,2]{1,0:T(8,128)S(1)}, u32[]{:S(2)}, u32[]{:S(2)}) collective-permute-start(f32[132,2]{1,0:T(8,128)S(1)} %get-tuple-element.17), channel_id=1, source_target_pairs={{1,0},{2,1},{3,2},{4,3},{5,4},{6,5},{7,6},{8,7},{9,8},{10,9},{11,1... | collective-permute-start | bytes 3176 | tf_op jit(solution)/shard_map/ppermute | solution.py:23
  590.3 7.2 %collective-permute-start.54 = (f32[132,2]{1,0:T(8,128)S(1)}, f32[132,2]{1,0:T(8,128)S(1)}, u32[]{:S(2)}, u32[]{:S(2)}) collective-permute-start(f32[132,2]{1,0:T(8,128)S(1)} %get-tuple-element.16), channel_id=1, source_target_pairs={{0,1},{1,2},{2,3},{3,4},{4,5},{5,6},{6,7},{7,8},{8,9},{9,10},{10,1... | collective-permute-start | bytes 3176 | tf_op jit(solution)/shard_map/ppermute | solution.py:22
  (14 other events, 256.7 us)
where the time goes:
time: 633 us; the launch traced here: 623 us
  blocking collectives  338 us (53%)
  starting transfers between devices  205 us (32%)
  matrix products  38.8 us (6%)
  between operations  18.3 us (3%)
  waiting for transfers between devices  12.2 us (2%)
  other arithmetic  9.16 us (1%)
    psum x2, blocking collectives, norm_sum(): return lax.psum(level_products(residual, residual), ('lat', 'lon'))  212 us
    ppermute x28, starting transfers between devices, with_halo(): before = lax.ppermute(last, axis, up)  148 us
    psum x1, blocking collectives, body(): curv_sum = lax.psum(curv_local, ('lat', 'lon'))  104 us
    ppermute x28, starting transfers between devices, with_halo(): after = lax.ppermute(first, axis, down)  50.6 us
    dot_general x40, matrix products, matmul(): jnp.dot(left, right, precision=highest, preferred_element_type=jnp.float32)  38.8 us
    all_to_all x1, blocking collectives, body(): lax.all_to_all(final_surface, 'lon', split_axis=0, concat_axis=1, tiled=T...  22 us
  transfers between devices with their start and end apart: 57, of which 5 were waited for; matrix products, arithmetic and copies ran while one was open for 4% of the time, Pallas kernels for 0%

commit v1 on v0

--- a/solution.py
+++ b/solution.py
@@ -118,7 +118,7 @@
             own_part = smoothed[1:-1, 1:-1]
             curv_local = curv_local + level_scales[apply_k] * jnp.sum(own_part * own_part)
         images, surface, curv_local = (images, apply_surface, curv_local)
-        curv_sum = lax.psum(curv_local, ("lat", "lon"))
+        curv_sum = lax.psum(lax.psum(curv_local, "lat"), "lon")
         step_size = res_norm / curv_sum
         solution = [solution[k] + step_size * search[k] for k in range(LEVELS)]
         surface_sum = surface_sum + step_size * surface

time: 633 us -> 719 us (1.14)
  blocking collectives: 338 us -> 426 us
    psum x1 -> x4, blocking collectives: 104 us -> 193 us  [body(): curv_sum = lax.psum(lax.psum(curv_local, 'lat'), 'lon')]
where the time goes in v1:
time: 719 us; the launch traced here: 709 us
  blocking collectives  426 us (59%)
  starting transfers between devices  203 us (28%)
  matrix products  38.8 us (5%)
  between operations  18.2 us (3%)
  waiting for transfers between devices  12.2 us (2%)
  other arithmetic  9.16 us (1%)
    psum x2, blocking collectives, norm_sum(): return lax.psum(level_products(residual, residual), ('lat', 'lon'))  212 us
    psum x4, blocking collectives, body(): curv_sum = lax.psum(lax.psum(curv_local, 'lat'), 'lon')  193 us
    ppermute x28, starting transfers between devices, with_halo(): before = lax.ppermute(last, axis, up)  147 us
    ppermute x28, starting transfers between devices, with_halo(): after = lax.ppermute(first, axis, down)  49.3 us
    dot_general x40, matrix products, matmul(): jnp.dot(left, right, precision=highest, preferred_element_type=jnp.float32)  38.8 us
    all_to_all x1, blocking collectives, body(): lax.all_to_all(final_surface, 'lon', split_axis=0, concat_axis=1, tiled=T...  20.9 us
  transfers between devices with their start and end apart: 57, of which 5 were waited for; matrix products, arithmetic and copies ran while one was open for 4% of the time, Pallas kernels for 0%

profile of v1, /device:TPU:98, one launch (start us, length us, event | category | flops | bytes accessed | tf_op | source)
XLA Modules:
  0.0 709.0 jit_solution(6027871833750890899)
XLA Ops:
  0.6 6.3 all-to-all-start
  7.4 9.0 %all-to-all-done = f32[8,16,512]{2,0,1:T(8,128)S(1)} async-done(((f32[8,16,512]{2,0,1:T(8,128)}), f32[8,16,512]{2,0,1:T(8,128)S(1)}, u32[]{:S(2)}, u32[]{:S(2)}) %all-to-all-start) | async-done | bytes 262176 | tf_op jit(solution)/shard_map/all_to_all | solution.py:62
  16.5 3.3 collective-permute-start.1
  19.9 4.6 collective-permute-start
  27.4 3.0 collective-permute-start.2
  32.9 2.5 collective-permute-start.5
  35.5 5.7 collective-permute-start.4
  45.1 6.0 collective-permute-start.12
  55.4 2.3 multiply_reduce_fusion.2
  59.1 2.7 collective-permute-start.6
  63.8 5.8 collective-permute-start.8
  74.9 8.3 %collective-permute-start.10 = (f32[36,2]{1,0:T(8,128)S(1)}, f32[36,2]{1,0:T(8,128)S(1)}, u32[]{:S(2)}, u32[]{:S(2)}) collective-permute-start(f32[36,2]{1,0:T(8,128)S(1)} %get-tuple-element.52), channel_id=1, source_target_pairs={{0,1},{1,2},{2,3},{3,4},{4,5},{5,6},{6,7},{7,8},{8,9},{9,10},{10,1... | collective-permute-start | bytes 872 | tf_op jit(solution)/shard_map/ppermute | solution.py:22
  83.9 5.8 collective-permute-start.16
  91.7 6.1 collective-permute-start.14
  103.7 6.2 collective-permute-start.18
  112.1 2.8 fusion.106
  116.8 6.0 collective-permute-start.20
  126.1 60.2 %psum.43 = f32[]{:T(128)} all-reduce(f32[]{:T(128)S(6)} %add.682), channel_id=1, replica_groups=mesh['lat'=32,'lon'=16] {'lat'}, use_global_device_ids=true, to_apply=%region_10.0 | all-reduce | flops 1 | bytes 8 | tf_op jit(solution)/shard_map/psum | solution.py:121
  187.6 3.0 collective-permute-start.22
  190.8 113.2 %psum.42 = f32[]{:T(128)} all-reduce(f32[]{:T(128)S(6)} %add.631), channel_id=1, replica_groups=mesh['lat'=32,'lon'=16] {'lat','lon'}, use_global_device_ids=true, to_apply=%region_4.0 | all-reduce | flops 1 | bytes 8 | tf_op jit(solution)/shard_map/psum | solution.py:58
  304.0 36.3 %psum.44 = f32[]{:T(128)} all-reduce(f32[]{:T(128)} %psum.43), channel_id=1, replica_groups=mesh['lat'=32,'lon'=16] {'lon'}, use_global_device_ids=true, to_apply=%region_11.0 | all-reduce | flops 1 | bytes 8 | tf_op jit(solution)/shard_map/psum | solution.py:121
  347.6 2.3 multiply_reduce_fusion
  352.6 98.8 %psum.45 = f32[]{:T(128)} all-reduce(f32[]{:T(128)S(6)} %add.701), channel_id=1, replica_groups=mesh['lat'=32,'lon'=16] {'lat','lon'}, use_global_device_ids=true, to_apply=%region_16.0 | all-reduce | flops 1 | bytes 8 | tf_op jit(solution)/shard_map/psum | solution.py:58
  452.8 2.5 collective-permute-start.33
  455.3 5.5 collective-permute-start.32
  462.7 6.0 collective-permute-start.24
  468.7 1.9 collective-permute-start.29
  472.1 3.0 collective-permute-start.26
  475.2 6.0 collective-permute-start.28
  481.2 2.1 collective-permute-start.37
  485.9 4.5 collective-permute-start.30
  491.8 5.8 collective-permute-start.36
  499.6 5.5 collective-permute-start.34
  511.0 5.8 collective-permute-start.38
  519.4 2.8 fusion.48
  524.7 60.2 %psum.46 = f32[]{:T(128)} all-reduce(f32[]{:T(128)S(6)} %add.724), channel_id=1, replica_groups=mesh['lat'=32,'lon'=16] {'lat'}, use_global_device_ids=true, to_apply=%region_22.0 | all-reduce | flops 1 | bytes 8 | tf_op jit(solution)/shard_map/psum | solution.py:121
  584.9 36.0 %psum.47 = f32[]{:T(128)} all-reduce(f32[]{:T(128)} %psum.46), channel_id=1, replica_groups=mesh['lat'=32,'lon'=16] {'lon'}, use_global_device_ids=true, to_apply=%region_23.0 | all-reduce | flops 1 | bytes 8 | tf_op jit(solution)/shard_map/psum | solution.py:121
  622.4 3.6 collective-permute-start.49
  626.0 5.2 collective-permute-start.48
  633.2 6.0 collective-permute-start.40
  642.6 3.0 collective-permute-start.42
  645.6 6.0 collective-permute-start.44
  654.6 6.0 collective-permute-start.52
  662.0 3.7 collective-permute-start.46
  667.1 5.8 collective-permute-start.50
  677.0 6.2 collective-permute-start.54
  684.9 2.2 fusion.7
  687.2 20.9 %all_to_all.38 = f32[16,8,512]{2,1,0:T(8,128)S(1)} all-to-all(f32[16,8,512]{2,1,0:T(8,128)S(1)} %fusion.7), channel_id=1, replica_groups=mesh['lat'=32,'lon'=16] {'lon'}, dimensions={0} | all-to-all | bytes 524288 | tf_op jit(solution)/shard_map/all_to_all | solution.py:131
  (224 shorter events, 74.2 us)
Async XLA Ops:
  0.6 15.8 %all-to-all-start = ((f32[8,16,512]{2,0,1:T(8,128)}), f32[8,16,512]{2,0,1:T(8,128)S(1)}, u32[]{:S(2)}, u32[]{:S(2)}) async-start(f32[8,16,512]{2,0,1:T(8,128)} %bitcast.39), calls=%async_computation | async-start | bytes 524288 | tf_op jit(solution)/shard_map/all_to_all | solution.py:62
  16.5 8.0 %collective-permute-start.1 = (f32[16,512]{1,0:T(8,128)S(1)}, f32[16,512]{1,0:T(8,128)S(1)}, u32[]{:S(2)}, u32[]{:S(2)}) collective-permute-start(f32[16,512]{1,0:T(8,128)S(1)} %get-tuple-element.29), channel_id=1, source_target_pairs={{16,0},{32,16},{48,32},{64,48},{80,64},{96,80},{112,96},{128,112},... | collective-permute-start | bytes 98312 | tf_op jit(solution)/shard_map/ppermute | solution.py:23
  32.9 26.1 %collective-permute-start.5 = (f32[2,64]{1,0:T(2,128)S(1)}, f32[2,64]{1,0:T(2,128)S(1)}, u32[]{:S(2)}, u32[]{:S(2)}) collective-permute-start(f32[2,64]{1,0:T(2,128)S(1)} %get-tuple-element.74), channel_id=1, source_target_pairs={{16,0},{32,16},{48,32},{64,48},{80,64},{96,80},{112,96},{128,112},... | collective-permute-start | bytes 1544 | tf_op jit(solution)/shard_map/ppermute | solution.py:23
  35.5 23.6 %collective-permute-start.4 = (f32[2,64]{1,0:T(2,128)S(1)}, f32[2,64]{1,0:T(2,128)S(1)}, u32[]{:S(2)}, u32[]{:S(2)}) collective-permute-start(f32[2,64]{1,0:T(2,128)S(1)} %get-tuple-element.73), channel_id=1, source_target_pairs={{0,16},{16,32},{32,48},{48,64},{64,80},{80,96},{96,112},{112,128},... | collective-permute-start | bytes 1544 | tf_op jit(solution)/shard_map/ppermute | solution.py:22
  43.2 47.0 %collective-permute-start.13 = (f32[2,256]{1,0:T(2,128)S(1)}, f32[2,256]{1,0:T(2,128)S(1)}, u32[]{:S(2)}, u32[]{:S(2)}) collective-permute-start(f32[2,256]{1,0:T(2,128)S(1)} %get-tuple-element.44), channel_id=1, source_target_pairs={{16,0},{32,16},{48,32},{64,48},{80,64},{96,80},{112,96},{128,112},... | collective-permute-start | bytes 6152 | tf_op jit(solution)/shard_map/ppermute | solution.py:23
  45.1 45.1 %collective-permute-start.12 = (f32[2,256]{1,0:T(2,128)S(1)}, f32[2,256]{1,0:T(2,128)S(1)}, u32[]{:S(2)}, u32[]{:S(2)}) collective-permute-start(f32[2,256]{1,0:T(2,128)S(1)} %get-tuple-element.43), channel_id=1, source_target_pairs={{0,16},{16,32},{32,48},{48,64},{64,80},{80,96},{96,112},{112,128},... | collective-permute-start | bytes 6152 | tf_op jit(solution)/shard_map/ppermute | solution.py:22
  52.8 20.0 %collective-permute-start.9 = (f32[2,128]{1,0:T(2,128)S(1)}, f32[2,128]{1,0:T(2,128)S(1)}, u32[]{:S(2)}, u32[]{:S(2)}) collective-permute-start(f32[2,128]{1,0:T(2,128)S(1)} %get-tuple-element.59), channel_id=1, source_target_pairs={{16,0},{32,16},{48,32},{64,48},{80,64},{96,80},{112,96},{128,112},... | collective-permute-start | bytes 3080 | tf_op jit(solution)/shard_map/ppermute | solution.py:23
  62.4 7.3 %collective-permute-start.7 = (f32[20,2]{1,0:T(8,128)S(1)}, f32[20,2]{1,0:T(8,128)S(1)}, u32[]{:S(2)}, u32[]{:S(2)}) collective-permute-start(f32[20,2]{1,0:T(8,128)S(1)} %get-tuple-element.68), channel_id=1, source_target_pairs={{1,0},{2,1},{3,2},{4,3},{5,4},{6,5},{7,6},{8,7},{9,8},{10,9},{11,1... | collective-permute-start | bytes 488 | tf_op jit(solution)/shard_map/ppermute | solution.py:23
  63.8 9.1 %collective-permute-start.8 = (f32[2,128]{1,0:T(2,128)S(1)}, f32[2,128]{1,0:T(2,128)S(1)}, u32[]{:S(2)}, u32[]{:S(2)}) collective-permute-start(f32[2,128]{1,0:T(2,128)S(1)} %get-tuple-element.58), channel_id=1, source_target_pairs={{0,16},{16,32},{32,48},{48,64},{64,80},{80,96},{96,112},{112,128},... | collective-permute-start | bytes 3080 | tf_op jit(solution)/shard_map/ppermute | solution.py:22
  69.7 32.6 %collective-permute-start.17 = (f32[2,512]{1,0:T(2,128)S(1)}, f32[2,512]{1,0:T(2,128)S(1)}, u32[]{:S(2)}, u32[]{:S(2)}) collective-permute-start(f32[2,512]{1,0:T(2,128)S(1)} %get-tuple-element.27), channel_id=1, source_target_pairs={{16,0},{32,16},{48,32},{64,48},{80,64},{96,80},{112,96},{128,112},... | collective-permute-start | bytes 12296 | tf_op jit(solution)/shard_map/ppermute | solution.py:23
  72.9 10.9 %collective-permute-start.11 = (f32[36,2]{1,0:T(8,128)S(1)}, f32[36,2]{1,0:T(8,128)S(1)}, u32[]{:S(2)}, u32[]{:S(2)}) collective-permute-start(f32[36,2]{1,0:T(8,128)S(1)} %get-tuple-element.53), channel_id=1, source_target_pairs={{1,0},{2,1},{3,2},{4,3},{5,4},{6,5},{7,6},{8,7},{9,8},{10,9},{11,1... | collective-permute-start | bytes 872 | tf_op jit(solution)/shard_map/ppermute | solution.py:23
  74.9 14.7 %collective-permute-start.10 = (f32[36,2]{1,0:T(8,128)S(1)}, f32[36,2]{1,0:T(8,128)S(1)}, u32[]{:S(2)}, u32[]{:S(2)}) collective-permute-start(f32[36,2]{1,0:T(8,128)S(1)} %get-tuple-element.52), channel_id=1, source_target_pairs={{0,1},{1,2},{2,3},{3,4},{4,5},{5,6},{6,7},{7,8},{8,9},{9,10},{10,1... | collective-permute-start | bytes 872 | tf_op jit(solution)/shard_map/ppermute | solution.py:22
  83.9 18.5 %collective-permute-start.16 = (f32[2,512]{1,0:T(2,128)S(1)}, f32[2,512]{1,0:T(2,128)S(1)}, u32[]{:S(2)}, u32[]{:S(2)}) collective-permute-start(f32[2,512]{1,0:T(2,128)S(1)} %get-tuple-element.26), channel_id=1, source_target_pairs={{0,16},{16,32},{32,48},{48,64},{64,80},{80,96},{96,112},{112,128},... | collective-permute-start | bytes 12296 | tf_op jit(solution)/shard_map/ppermute | solution.py:22
  90.4 8.7 %collective-permute-start.15 = (f32[68,2]{1,0:T(8,128)S(1)}, f32[68,2]{1,0:T(8,128)S(1)}, u32[]{:S(2)}, u32[]{:S(2)}) collective-permute-start(f32[68,2]{1,0:T(8,128)S(1)} %get-tuple-element.38), channel_id=1, source_target_pairs={{1,0},{2,1},{3,2},{4,3},{5,4},{6,5},{7,6},{8,7},{9,8},{10,9},{11,1... | collective-permute-start | bytes 1640 | tf_op jit(solution)/shard_map/ppermute | solution.py:23
  91.7 7.4 %collective-permute-start.14 = (f32[68,2]{1,0:T(8,128)S(1)}, f32[68,2]{1,0:T(8,128)S(1)}, u32[]{:S(2)}, u32[]{:S(2)}) collective-permute-start(f32[68,2]{1,0:T(8,128)S(1)} %get-tuple-element.37), channel_id=1, source_target_pairs={{0,1},{1,2},{2,3},{3,4},{4,5},{5,6},{6,7},{7,8},{8,9},{9,10},{10,1... | collective-permute-start | bytes 1640 | tf_op jit(solution)/shard_map/ppermute | solution.py:22
  102.4 8.9 %collective-permute-start.19 = (f32[132,2]{1,0:T(8,128)S(1)}, f32[132,2]{1,0:T(8,128)S(1)}, u32[]{:S(2)}, u32[]{:S(2)}) collective-permute-start(f32[132,2]{1,0:T(8,128)S(1)} %get-tuple-element.19), channel_id=1, source_target_pairs={{1,0},{2,1},{3,2},{4,3},{5,4},{6,5},{7,6},{8,7},{9,8},{10,9},{11,1... | collective-permute-start | bytes 3176 | tf_op jit(solution)/shard_map/ppermute | solution.py:23
  103.7 7.6 %collective-permute-start.18 = (f32[132,2]{1,0:T(8,128)S(1)}, f32[132,2]{1,0:T(8,128)S(1)}, u32[]{:S(2)}, u32[]{:S(2)}) collective-permute-start(f32[132,2]{1,0:T(8,128)S(1)} %get-tuple-element.18), channel_id=1, source_target_pairs={{0,1},{1,2},{2,3},{3,4},{4,5},{5,6},{6,7},{7,8},{8,9},{9,10},{10,1... | collective-permute-start | bytes 3176 | tf_op jit(solution)/shard_map/ppermute | solution.py:22
  114.9 71.3 %collective-permute-start.21 = (f32[16,512]{1,0:T(8,128)S(1)}, f32[16,512]{1,0:T(8,128)S(1)}, u32[]{:S(2)}, u32[]{:S(2)}) collective-permute-start(f32[16,512]{1,0:T(8,128)S(1)} %get-tuple-element.25), channel_id=1, source_target_pairs={{16,0},{32,16},{48,32},{64,48},{80,64},{96,80},{112,96},{128,112},... | collective-permute-start | bytes 98312 | tf_op jit(solution)/shard_map/ppermute | solution.py:23
  116.8 69.4 %collective-permute-start.20 = (f32[16,512]{1,0:T(8,128)S(1)}, f32[16,512]{1,0:T(8,128)S(1)}, u32[]{:S(2)}, u32[]{:S(2)}) collective-permute-start(f32[16,512]{1,0:T(8,128)S(1)} %get-tuple-element.24), channel_id=1, source_target_pairs={{0,16},{16,32},{32,48},{48,64},{64,80},{80,96},{96,112},{112,128},... | collective-permute-start | bytes 98312 | tf_op jit(solution)/shard_map/ppermute | solution.py:22
  186.3 155.3 %collective-permute-start.23 = (f32[160,16]{1,0:T(8,128)S(1)}, f32[160,16]{1,0:T(8,128)S(1)}, u32[]{:S(2)}, u32[]{:S(2)}) collective-permute-start(f32[160,16]{1,0:T(8,128)S(1)} %get-tuple-element.11), channel_id=1, source_target_pairs={{1,0},{2,1},{3,2},{4,3},{5,4},{6,5},{7,6},{8,7},{9,8},{10,9},{11,1... | collective-permute-start | bytes 30728 | tf_op jit(solution)/shard_map/ppermute | solution.py:23
  187.6 154.0 %collective-permute-start.22 = (f32[160,16]{1,0:T(8,128)S(1)}, f32[160,16]{1,0:T(8,128)S(1)}, u32[]{:S(2)}, u32[]{:S(2)}) collective-permute-start(f32[160,16]{1,0:T(8,128)S(1)} %get-tuple-element.10), channel_id=1, source_target_pairs={{0,1},{1,2},{2,3},{3,4},{4,5},{5,6},{6,7},{7,8},{8,9},{9,10},{10,1... | collective-permute-start | bytes 30728 | tf_op jit(solution)/shard_map/ppermute | solution.py:22
  452.8 45.4 %collective-permute-start.33 = (f32[2,256]{1,0:T(2,128)S(1)}, f32[2,256]{1,0:T(2,128)S(1)}, u32[]{:S(2)}, u32[]{:S(2)}) collective-permute-start(f32[2,256]{1,0:T(2,128)S(1)} %get-tuple-element.42), channel_id=1, source_target_pairs={{16,0},{32,16},{48,32},{64,48},{80,64},{96,80},{112,96},{128,112},... | collective-permute-start | bytes 6152 | tf_op jit(solution)/shard_map/ppermute | solution.py:23
  455.3 42.9 %collective-permute-start.32 = (f32[2,256]{1,0:T(2,128)S(1)}, f32[2,256]{1,0:T(2,128)S(1)}, u32[]{:S(2)}, u32[]{:S(2)}) collective-permute-start(f32[2,256]{1,0:T(2,128)S(1)} %get-tuple-element.41), channel_id=1, source_target_pairs={{0,16},{16,32},{32,48},{48,64},{64,80},{80,96},{96,112},{112,128},... | collective-permute-start | bytes 6152 | tf_op jit(solution)/shard_map/ppermute | solution.py:22
  460.8 10.0 %collective-permute-start.25 = (f32[2,64]{1,0:T(2,128)S(1)}, f32[2,64]{1,0:T(2,128)S(1)}, u32[]{:S(2)}, u32[]{:S(2)}) collective-permute-start(f32[2,64]{1,0:T(2,128)S(1)} %get-tuple-element.72), channel_id=1, source_target_pairs={{16,0},{32,16},{48,32},{64,48},{80,64},{96,80},{112,96},{128,112},... | collective-permute-start | bytes 1544 | tf_op jit(solution)/shard_map/ppermute | solution.py:23
  462.7 8.1 %collective-permute-start.24 = (f32[2,64]{1,0:T(2,128)S(1)}, f32[2,64]{1,0:T(2,128)S(1)}, u32[]{:S(2)}, u32[]{:S(2)}) collective-permute-start(f32[2,64]{1,0:T(2,128)S(1)} %get-tuple-element.71), channel_id=1, source_target_pairs={{0,16},{16,32},{32,48},{48,64},{64,80},{80,96},{96,112},{112,128},... | collective-permute-start | bytes 1544 | tf_op jit(solution)/shard_map/ppermute | solution.py:22
  468.7 15.7 %collective-permute-start.29 = (f32[2,128]{1,0:T(2,128)S(1)}, f32[2,128]{1,0:T(2,128)S(1)}, u32[]{:S(2)}, u32[]{:S(2)}) collective-permute-start(f32[2,128]{1,0:T(2,128)S(1)} %get-tuple-element.57), channel_id=1, source_target_pairs={{16,0},{32,16},{48,32},{64,48},{80,64},{96,80},{112,96},{128,112},... | collective-permute-start | bytes 3080 | tf_op jit(solution)/shard_map/ppermute | solution.py:23
  472.1 9.1 %collective-permute-start.26 = (f32[20,2]{1,0:T(8,128)S(1)}, f32[20,2]{1,0:T(8,128)S(1)}, u32[]{:S(2)}, u32[]{:S(2)}) collective-permute-start(f32[20,2]{1,0:T(8,128)S(1)} %get-tuple-element.65), channel_id=1, source_target_pairs={{0,1},{1,2},{2,3},{3,4},{4,5},{5,6},{6,7},{7,8},{8,9},{9,10},{10,1... | collective-permute-start | bytes 488 | tf_op jit(solution)/shard_map/ppermute | solution.py:22
  475.2 9.3 %collective-permute-start.28 = (f32[2,128]{1,0:T(2,128)S(1)}, f32[2,128]{1,0:T(2,128)S(1)}, u32[]{:S(2)}, u32[]{:S(2)}) collective-permute-start(f32[2,128]{1,0:T(2,128)S(1)} %get-tuple-element.56), channel_id=1, source_target_pairs={{0,16},{16,32},{32,48},{48,64},{64,80},{80,96},{96,112},{112,128},... | collective-permute-start | bytes 3080 | tf_op jit(solution)/shard_map/ppermute | solution.py:22
  481.2 28.4 %collective-permute-start.37 = (f32[2,512]{1,0:T(2,128)S(1)}, f32[2,512]{1,0:T(2,128)S(1)}, u32[]{:S(2)}, u32[]{:S(2)}) collective-permute-start(f32[2,512]{1,0:T(2,128)S(1)} %get-tuple-element.23), channel_id=1, source_target_pairs={{16,0},{32,16},{48,32},{64,48},{80,64},{96,80},{112,96},{128,112},... | collective-permute-start | bytes 12296 | tf_op jit(solution)/shard_map/ppermute | solution.py:23
  484.6 7.2 %collective-permute-start.31 = (f32[36,2]{1,0:T(8,128)S(1)}, f32[36,2]{1,0:T(8,128)S(1)}, u32[]{:S(2)}, u32[]{:S(2)}) collective-permute-start(f32[36,2]{1,0:T(8,128)S(1)} %get-tuple-element.51), channel_id=1, source_target_pairs={{1,0},{2,1},{3,2},{4,3},{5,4},{6,5},{7,6},{8,7},{9,8},{10,9},{11,1... | collective-permute-start | bytes 872 | tf_op jit(solution)/shard_map/ppermute | solution.py:23
  485.9 11.7 %collective-permute-start.30 = (f32[36,2]{1,0:T(8,128)S(1)}, f32[36,2]{1,0:T(8,128)S(1)}, u32[]{:S(2)}, u32[]{:S(2)}) collective-permute-start(f32[36,2]{1,0:T(8,128)S(1)} %get-tuple-element.50), channel_id=1, source_target_pairs={{0,1},{1,2},{2,3},{3,4},{4,5},{5,6},{6,7},{7,8},{8,9},{9,10},{10,1... | collective-permute-start | bytes 872 | tf_op jit(solution)/shard_map/ppermute | solution.py:22
  491.8 17.8 %collective-permute-start.36 = (f32[2,512]{1,0:T(2,128)S(1)}, f32[2,512]{1,0:T(2,128)S(1)}, u32[]{:S(2)}, u32[]{:S(2)}) collective-permute-start(f32[2,512]{1,0:T(2,128)S(1)} %get-tuple-element.22), channel_id=1, source_target_pairs={{0,16},{16,32},{32,48},{48,64},{64,80},{80,96},{96,112},{112,128},... | collective-permute-start | bytes 12296 | tf_op jit(solution)/shard_map/ppermute | solution.py:22
  498.3 8.2 %collective-permute-start.35 = (f32[68,2]{1,0:T(8,128)S(1)}, f32[68,2]{1,0:T(8,128)S(1)}, u32[]{:S(2)}, u32[]{:S(2)}) collective-permute-start(f32[68,2]{1,0:T(8,128)S(1)} %get-tuple-element.36), channel_id=1, source_target_pairs={{1,0},{2,1},{3,2},{4,3},{5,4},{6,5},{7,6},{8,7},{9,8},{10,9},{11,1... | collective-permute-start | bytes 1640 | tf_op jit(solution)/shard_map/ppermute | solution.py:23
  509.7 8.5 %collective-permute-start.39 = (f32[132,2]{1,0:T(8,128)S(1)}, f32[132,2]{1,0:T(8,128)S(1)}, u32[]{:S(2)}, u32[]{:S(2)}) collective-permute-start(f32[132,2]{1,0:T(8,128)S(1)} %get-tuple-element.17), channel_id=1, source_target_pairs={{1,0},{2,1},{3,2},{4,3},{5,4},{6,5},{7,6},{8,7},{9,8},{10,9},{11,1... | collective-permute-start | bytes 3176 | tf_op jit(solution)/shard_map/ppermute | solution.py:23
  511.0 7.2 %collective-permute-start.38 = (f32[132,2]{1,0:T(8,128)S(1)}, f32[132,2]{1,0:T(8,128)S(1)}, u32[]{:S(2)}, u32[]{:S(2)}) collective-permute-start(f32[132,2]{1,0:T(8,128)S(1)} %get-tuple-element.16), channel_id=1, source_target_pairs={{0,1},{1,2},{2,3},{3,4},{4,5},{5,6},{6,7},{7,8},{8,9},{9,10},{10,1... | collective-permute-start | bytes 3176 | tf_op jit(solution)/shard_map/ppermute | solution.py:22
  622.4 39.7 %collective-permute-start.49 = (f32[2,256]{1,0:T(2,128)S(1)}, f32[2,256]{1,0:T(2,128)S(1)}, u32[]{:S(2)}, u32[]{:S(2)}) collective-permute-start(f32[2,256]{1,0:T(2,128)S(1)} %get-tuple-element.40), channel_id=1, source_target_pairs={{16,0},{32,16},{48,32},{64,48},{80,64},{96,80},{112,96},{128,112},... | collective-permute-start | bytes 6152 | tf_op jit(solution)/shard_map/ppermute | solution.py:23
  626.0 39.7 %collective-permute-start.48 = (f32[2,256]{1,0:T(2,128)S(1)}, f32[2,256]{1,0:T(2,128)S(1)}, u32[]{:S(2)}, u32[]{:S(2)}) collective-permute-start(f32[2,256]{1,0:T(2,128)S(1)} %get-tuple-element.39), channel_id=1, source_target_pairs={{0,16},{16,32},{32,48},{48,64},{64,80},{80,96},{96,112},{112,128},... | collective-permute-start | bytes 6152 | tf_op jit(solution)/shard_map/ppermute | solution.py:22
  631.2 9.9 %collective-permute-start.41 = (f32[2,64]{1,0:T(2,128)S(1)}, f32[2,64]{1,0:T(2,128)S(1)}, u32[]{:S(2)}, u32[]{:S(2)}) collective-permute-start(f32[2,64]{1,0:T(2,128)S(1)} %get-tuple-element.70), channel_id=1, source_target_pairs={{16,0},{32,16},{48,32},{64,48},{80,64},{96,80},{112,96},{128,112},... | collective-permute-start | bytes 1544 | tf_op jit(solution)/shard_map/ppermute | solution.py:23
  633.2 8.0 %collective-permute-start.40 = (f32[2,64]{1,0:T(2,128)S(1)}, f32[2,64]{1,0:T(2,128)S(1)}, u32[]{:S(2)}, u32[]{:S(2)}) collective-permute-start(f32[2,64]{1,0:T(2,128)S(1)} %get-tuple-element.69), channel_id=1, source_target_pairs={{0,16},{16,32},{32,48},{48,64},{64,80},{80,96},{96,112},{112,128},... | collective-permute-start | bytes 1544 | tf_op jit(solution)/shard_map/ppermute | solution.py:22
  639.2 15.4 %collective-permute-start.45 = (f32[2,128]{1,0:T(2,128)S(1)}, f32[2,128]{1,0:T(2,128)S(1)}, u32[]{:S(2)}, u32[]{:S(2)}) collective-permute-start(f32[2,128]{1,0:T(2,128)S(1)} %get-tuple-element.55), channel_id=1, source_target_pairs={{16,0},{32,16},{48,32},{64,48},{80,64},{96,80},{112,96},{128,112},... | collective-permute-start | bytes 3080 | tf_op jit(solution)/shard_map/ppermute | solution.py:23
  642.6 9.1 %collective-permute-start.42 = (f32[20,2]{1,0:T(8,128)S(1)}, f32[20,2]{1,0:T(8,128)S(1)}, u32[]{:S(2)}, u32[]{:S(2)}) collective-permute-start(f32[20,2]{1,0:T(8,128)S(1)} %get-tuple-element.60), channel_id=1, source_target_pairs={{0,1},{1,2},{2,3},{3,4},{4,5},{5,6},{6,7},{7,8},{8,9},{9,10},{10,1... | collective-permute-start | bytes 488 | tf_op jit(solution)/shard_map/ppermute | solution.py:22
  645.6 15.0 %collective-permute-start.44 = (f32[2,128]{1,0:T(2,128)S(1)}, f32[2,128]{1,0:T(2,128)S(1)}, u32[]{:S(2)}, u32[]{:S(2)}) collective-permute-start(f32[2,128]{1,0:T(2,128)S(1)} %get-tuple-element.54), channel_id=1, source_target_pairs={{0,16},{16,32},{32,48},{48,64},{64,80},{80,96},{96,112},{112,128},... | collective-permute-start | bytes 3080 | tf_op jit(solution)/shard_map/ppermute | solution.py:22
  651.7 24.0 %collective-permute-start.53 = (f32[2,512]{1,0:T(2,128)S(1)}, f32[2,512]{1,0:T(2,128)S(1)}, u32[]{:S(2)}, u32[]{:S(2)}) collective-permute-start(f32[2,512]{1,0:T(2,128)S(1)} %get-tuple-element.21), channel_id=1, source_target_pairs={{16,0},{32,16},{48,32},{64,48},{80,64},{96,80},{112,96},{128,112},... | collective-permute-start | bytes 12296 | tf_op jit(solution)/shard_map/ppermute | solution.py:23
  654.6 21.0 %collective-permute-start.52 = (f32[2,512]{1,0:T(2,128)S(1)}, f32[2,512]{1,0:T(2,128)S(1)}, u32[]{:S(2)}, u32[]{:S(2)}) collective-permute-start(f32[2,512]{1,0:T(2,128)S(1)} %get-tuple-element.20), channel_id=1, source_target_pairs={{0,16},{16,32},{32,48},{48,64},{64,80},{80,96},{96,112},{112,128},... | collective-permute-start | bytes 12296 | tf_op jit(solution)/shard_map/ppermute | solution.py:22
  662.0 10.9 %collective-permute-start.46 = (f32[36,2]{1,0:T(8,128)S(1)}, f32[36,2]{1,0:T(8,128)S(1)}, u32[]{:S(2)}, u32[]{:S(2)}) collective-permute-start(f32[36,2]{1,0:T(8,128)S(1)} %get-tuple-element.48), channel_id=1, source_target_pairs={{0,1},{1,2},{2,3},{3,4},{4,5},{5,6},{6,7},{7,8},{8,9},{9,10},{10,1... | collective-permute-start | bytes 872 | tf_op jit(solution)/shard_map/ppermute | solution.py:22
  665.8 7.5 %collective-permute-start.51 = (f32[68,2]{1,0:T(8,128)S(1)}, f32[68,2]{1,0:T(8,128)S(1)}, u32[]{:S(2)}, u32[]{:S(2)}) collective-permute-start(f32[68,2]{1,0:T(8,128)S(1)} %get-tuple-element.34), channel_id=1, source_target_pairs={{1,0},{2,1},{3,2},{4,3},{5,4},{6,5},{7,6},{8,7},{9,8},{10,9},{11,1... | collective-permute-start | bytes 1640 | tf_op jit(solution)/shard_map/ppermute | solution.py:23
  675.7 8.5 %collective-permute-start.55 = (f32[132,2]{1,0:T(8,128)S(1)}, f32[132,2]{1,0:T(8,128)S(1)}, u32[]{:S(2)}, u32[]{:S(2)}) collective-permute-start(f32[132,2]{1,0:T(8,128)S(1)} %get-tuple-element.15), channel_id=1, source_target_pairs={{1,0},{2,1},{3,2},{4,3},{5,4},{6,5},{7,6},{8,7},{9,8},{10,9},{11,1... | collective-permute-start | bytes 3176 | tf_op jit(solution)/shard_map/ppermute | solution.py:23
  677.0 7.2 %collective-permute-start.54 = (f32[132,2]{1,0:T(8,128)S(1)}, f32[132,2]{1,0:T(8,128)S(1)}, u32[]{:S(2)}, u32[]{:S(2)}) collective-permute-start(f32[132,2]{1,0:T(8,128)S(1)} %get-tuple-element.14), channel_id=1, source_target_pairs={{0,1},{1,2},{2,3},{3,4},{4,5},{5,6},{6,7},{7,8},{8,9},{9,10},{10,1... | collective-permute-start | bytes 3176 | tf_op jit(solution)/shard_map/ppermute | solution.py:22
  (14 other events, 258.9 us)
